TPU v7x, 32 devices: a whole 2x2x4 slice. The times are simulated.
32 devices in a mesh: grp: 2 (over x), probe: 8 (over z, y), beam: 2 (over core).
Axes of the slice: x: 2, y: 2, z: 4, core: 2. Of those that a mesh axis runs over, the one named last changes fastest.
Arguments:
- smatrix: bfloat16 [8192, 8, 512], P(('grp', 'beam'), 'probe'), parts along dimension 0, may hold values from -0.09375 to 0.09375
- aperture: float32 [4096], P('beam'), may hold values from 0.5 to 1.5
- aberration: float32 [4096], P('beam'), may hold values from -3.140625 to 3.140625
- beam_k: int32 [2, 4096], P(None, 'beam'), may hold values from -32 to 31, as said below
- probe_pos: int32 [2, 2048], P(None, 'probe'), may hold values from 0 to 1023
- patches: bfloat16 [128, 512], P(('grp', 'probe')), parts along dimension 0, may hold values from -6 to 6
- patch_col: int32 [128], P('grp'), parts along dimension 0, may hold values from 0 to 7, never falling along the last dimension, each value on 1 to 32 neighbouring positions
Outputs:
- ionization: float32 [16, 2048], P('grp', ('probe', 'beam')), parts along dimension 0
There are 2 independent parts, one for each index of `grp`. A program takes and returns all parts, laid end to end along the dimension named above; an argument that names none is the same for every part. Nothing has to cross between parts.
Inputs may be any that keep to these rules, and one draw needn't show every extreme that they name: `patch_col`: patches are ordered by atom column; each of the 8 columns has 1 to 32 patches, and some column has exactly 32. `beam_k`: no two beams have the same pair of indices.
All inputs are finite; a program needn't handle non-finite values.
Results may differ from a plain program's by a relative error of at most 0.005.
Values may be sent and summed in bfloat16 or wider, within the bound.
A program may use at most 128 MiB of HBM per device.

v0:
```python
import math
import jax
import jax.numpy as jnp
from jax import lax
from jax.sharding import PartitionSpec as P

PSIDE = 16
GRID = 1024


def coefficients(beam_k, beam_cos, beam_sin, positions):
    turn_count = (
        positions[0][:, None] * beam_k[0][None, :] + positions[1][:, None] * beam_k[1][None, :]
        & GRID - 1
    )
    quarter = GRID // 4
    quadrant = lax.shift_right_arithmetic(turn_count + quarter // 2, quarter.bit_length() - 1)
    resid = (turn_count - quadrant * quarter).astype(jnp.float32) * (2.0 * math.pi / GRID)
    sq = resid * resid
    sin_r = resid + resid * sq * (
        -1.0 / 6 + sq * (1.0 / 120 + sq * (-1.0 / 5040 + sq * (1.0 / 362880)))
    )
    cos_r = 1.0 + sq * (-0.5 + sq * (1.0 / 24 + sq * (-1.0 / 720 + sq * (1.0 / 40320))))
    odd = quadrant & 1 == 1
    cos_mag = jnp.where(odd, sin_r, cos_r)
    sin_mag = jnp.where(odd, cos_r, sin_r)
    cos_t = jnp.where(quadrant + 1 & 2 != 0, -cos_mag, cos_mag)
    sin_t = jnp.where(quadrant & 2 != 0, -sin_mag, sin_mag)
    real_coef = (beam_cos[None, :] * cos_t - beam_sin[None, :] * sin_t).astype(jnp.bfloat16)
    imag_coef = (-(beam_sin[None, :] * cos_t + beam_cos[None, :] * sin_t)).astype(jnp.bfloat16)
    return (real_coef, imag_coef)


def detector(edge_count):
    half_side = edge_count // 2
    pixel_index = jnp.arange(edge_count * edge_count, dtype=jnp.int32)
    mode_index = jnp.arange(edge_count * half_side, dtype=jnp.int32)
    row_off = pixel_index // edge_count
    col_off = pixel_index % edge_count
    freq_first = mode_index // half_side - half_side
    freq_second = mode_index % half_side - edge_count // 4
    turn_count = jnp.mod(
        row_off[:, None] * freq_first[None, :] + col_off[:, None] * freq_second[None, :], edge_count
    )
    angle_value = 2.0 * math.pi / edge_count * turn_count.astype(jnp.float32)
    real_part = jnp.cos(angle_value)
    imag_part = -jnp.sin(angle_value)
    upper_rows = jnp.concatenate([real_part, imag_part], axis=1)
    lower_rows = jnp.concatenate([-imag_part, real_part], axis=1)
    return jnp.concatenate([upper_rows, lower_rows], axis=0).astype(jnp.bfloat16)


def patch_energy(picked, pot_rows, det_table):
    half_width = pot_rows.shape[-1] // 2
    psi_re = picked[..., :half_width].astype(jnp.float32)
    psi_im = picked[..., half_width:].astype(jnp.float32)
    pot_re = pot_rows[:, :half_width].astype(jnp.float32)
    pot_im = pot_rows[:, half_width:].astype(jnp.float32)
    wave_out = jnp.concatenate(
        [psi_re * pot_re - psi_im * pot_im, psi_re * pot_im + psi_im * pot_re], axis=-1
    ).astype(jnp.bfloat16)
    projected = jnp.einsum("rjx,xq->rjq", wave_out, det_table, preferred_element_type=jnp.float32)
    return jnp.sum(projected * projected, axis=-1) / float(half_width * (det_table.shape[1] // 2))


def combine(beam_terms):
    half_width = beam_terms.shape[-1] // 2
    return jnp.concatenate(
        [
            beam_terms[0, ..., :half_width] - beam_terms[1, ..., half_width:],
            beam_terms[0, ..., half_width:] + beam_terms[1, ..., :half_width],
        ],
        axis=-1,
    )


def spread_patches(psi, all_patches, patch_col, det_table):
    patch_total = all_patches.shape[0]
    group_size = math.gcd(patch_total, 16)
    column_count = psi.shape[1]
    col_groups = patch_col.reshape(patch_total // group_size, group_size)
    pot_groups = all_patches.reshape(patch_total // group_size, group_size, all_patches.shape[1])
    col_range = jnp.arange(column_count, dtype=jnp.int32)

    def add_block(running, blk_pair):
        col_ids, pot_rows = blk_pair
        picked = jnp.take(psi, col_ids, axis=1)
        energy = patch_energy(picked, pot_rows, det_table)
        onehot = (col_ids[:, None] == col_range[None, :]).astype(jnp.float32)
        return (
            running + jnp.einsum("rj,jc->cr", energy, onehot, precision=lax.Precision.HIGHEST),
            None,
        )

    running, _ = lax.scan(
        add_block, jnp.zeros((column_count, psi.shape[0]), jnp.float32), (col_groups, pot_groups)
    )
    return running


def apply_patches(psi_own, all_patches, patch_col, det_table):
    traded = lax.all_to_all(psi_own, "probe", split_axis=0, concat_axis=2, tiled=True)
    return spread_patches(traded[0], all_patches, patch_col, det_table)


def shards(smatrix, aperture, aberration, beam_k, probe_pos, patches, patch_col):
    probe_count = lax.axis_size("probe")
    beam_count = lax.axis_size("beam")
    all_patches = lax.all_gather(patches, "probe", axis=0, tiled=True)
    det_table = detector(PSIDE)
    col_dev = smatrix.shape[1]
    width_two = smatrix.shape[2]
    full_matrix = lax.all_gather(smatrix, "beam", axis=0, tiled=True)
    full_cos = lax.all_gather(aperture * jnp.cos(aberration), "beam", axis=0, tiled=True)
    full_sin = lax.all_gather(aperture * jnp.sin(aberration), "beam", axis=0, tiled=True)
    full_k = lax.all_gather(beam_k, "beam", axis=1, tiled=True)
    all_pos = lax.all_gather(probe_pos, "probe", axis=1, tiled=True)
    all_pos, all_patches = lax.optimization_barrier((all_pos, all_patches))
    probe_total = all_pos.shape[1]
    half_probes = probe_total // (beam_count * probe_count)
    split_pos = all_pos.reshape(2, probe_count, beam_count, half_probes)
    mine = lax.dynamic_slice_in_dim(split_pos, lax.axis_index("beam"), 1, 2).reshape(
        2, probe_count * half_probes
    )
    real_coef, imag_coef = coefficients(full_k, full_cos, full_sin, mine)
    beam_terms = jnp.einsum(
        "kpb,bcx->kpcx",
        jnp.stack([real_coef, imag_coef]),
        full_matrix,
        preferred_element_type=jnp.float32,
    )
    psi_own = (
        combine(beam_terms)
        .astype(jnp.bfloat16)
        .reshape(probe_count, half_probes, col_dev, width_two)
    )
    return apply_patches(psi_own, all_patches, patch_col, det_table)


def solution(mesh):
    placed = (
        P(("grp", "beam"), "probe", None),
        P("beam"),
        P("beam"),
        P(None, "beam"),
        P(None, "probe"),
        P(("grp", "probe"), None),
        P("grp"),
    )
    return jax.shard_map(
        shards, mesh=mesh, in_specs=placed, out_specs=P("grp", ("probe", "beam")), check_vma=False
    )
```

profile of v0, /device:TPU:0, one launch (start us, length us, event | category | flops | bytes accessed | tf_op | source)
XLA Modules:
  0.0 168.4 jit_solution(5774982528233616721)
XLA Ops:
  6.5 0.7 all-gather.2.cloned.1.call-update
  7.3 32.6 %all_gather.20 = bf16[64,512]{1,0:T(8,128)(2,1)S(1)} all-gather(bf16[8,512]{1,0:T(8,128)(2,1)} %param.14), channel_id=1, replica_groups=mesh['grp'=2,'probe'=8,'beam'=2] {'probe'}, dimensions={0}, use_global_device_ids=true | all-gather | bytes 73728 | tf_op jit(solution)/shard_map/all_gather | solution.py:109
  39.8 26.2 %all_gather.19 = s32[2,2048]{1,0:T(2,128)S(1)} all-gather(s32[2,256]{1,0:T(2,128)} %param.13), channel_id=1, replica_groups=mesh['grp'=2,'probe'=8,'beam'=2] {'probe'}, dimensions={1}, use_global_device_ids=true | all-gather | bytes 18432 | tf_op jit(solution)/shard_map/all_gather | solution.py:117
  66.1 2.0 %all_gather.21 = s32[2,4096]{1,0:T(2,128)S(1)} all-gather(s32[2,2048]{1,0:T(2,128)} %param.12), channel_id=1, replica_groups=mesh['grp'=2,'probe'=8,'beam'=2] {'beam'}, dimensions={1}, use_global_device_ids=true | all-gather | bytes 49152 | tf_op jit(solution)/shard_map/all_gather | solution.py:116
  68.2 0.8 cosine_multiply_fusion
  68.9 1.8 %all_gather.18 = f32[4096]{0:T(1024)S(1)} all-gather(f32[2048]{0:T(1024)S(1)} %get-tuple-element.96), channel_id=1, replica_groups=mesh['grp'=2,'probe'=8,'beam'=2] {'beam'}, dimensions={0}, use_global_device_ids=true | all-gather | bytes 24576 | tf_op jit(solution)/shard_map/all_gather | solution.py:114
  70.8 1.8 %all_gather.22 = f32[4096]{0:T(1024)S(1)} all-gather(f32[2048]{0:T(1024)S(1)} %get-tuple-element.97), channel_id=1, replica_groups=mesh['grp'=2,'probe'=8,'beam'=2] {'beam'}, dimensions={0}, use_global_device_ids=true | all-gather | bytes 24576 | tf_op jit(solution)/shard_map/all_gather | solution.py:115
  72.6 28.6 %subtract_convert_fusion = (bf16[1,1024,4096]{2,1,0:T(8,128)(2,1)}, bf16[1,1024,4096]{2,1,0:T(8,128)(2,1)}) fusion(f32[4096]{0:T(1024)S(1)} %all_gather.22, f32[4096]{0:T(1024)S(1)} %all_gather.18, s32[4096]{0:T(1024)S(1)} %bitcast.53, s32[1024]{0:T(1024)S(1)} %bitcast.55, s32[4096]{0:T(1024)S(1)} %bitcast.52, s32[1024]{0:T(1024)S(1)} %bitcast.54), kind=kLoop, calls=%fused_computation.60 | loop fusion | flops 209715200 | bytes 16850944 | tf_op jit(solution)/shard_map/convert_element_type | solution.py:29
  101.2 13.2 %fusion.37 = f32[2,1024,1,512]{3,1,0,2:T(8,128)S(1)} fusion(bf16[4096,1,512]{2,0,1:T(8,128)(2,1)} %all-gather.2.cloned.1.call-done, bf16[1,1024,4096]{2,1,0:T(8,128)(2,1)} %get-tuple-element.91, bf16[1,1024,4096]{2,1,0:T(8,128)(2,1)} %get-tuple-element.90), kind=kOutput, calls=%fused_computation.68 | convolution fusion | flops 8598323200 | bytes 25165824 | tf_op jit(solution)/shard_map/kpb,bcx->kpcx/dot_general | solution.py:126
  114.7 1.1 pad_maximum_fusion
  115.7 3.9 %all-to-all-start = ((bf16[8,128,1,512]{3,1,2,0:T(8,128)(2,1)}), bf16[8,128,1,512]{3,1,2,0:T(8,128)(2,1)S(1)}, u32[]{:S(2)}, u32[]{:S(2)}) async-start(bf16[8,128,1,512]{3,1,2,0:T(8,128)(2,1)} %pad_maximum_fusion), calls=%async_computation | async-start | bytes 2097152 | tf_op jit(solution)/shard_map/all_to_all | solution.py:102
  120.4 25.3 %all-to-all-done = bf16[8,128,1,512]{3,1,2,0:T(8,128)(2,1)S(1)} async-done(((bf16[8,128,1,512]{3,1,2,0:T(8,128)(2,1)}), bf16[8,128,1,512]{3,1,2,0:T(8,128)(2,1)S(1)}, u32[]{:S(2)}, u32[]{:S(2)}) %all-to-all-start) | async-done | bytes 1048608 | tf_op jit(solution)/shard_map/all_to_all | solution.py:102
  145.7 15.3 %while.11 = (s32[]{:T(128)}, f32[8,128]{1,0:T(8,128)S(1)}, s32[4,16]{1,0:T(4,128)S(1)}, bf16[128,8,512]{2,0,1:T(8,128)(2,1)S(1)}, bf16[4,16,512]{2,1,0:T(8,128)(...) while((s32[]{:T(128)}, f32[8,128]{1,0:T(8,128)S(1)}, s32[4,16]{1,0:T(4,128)S(1)}, ...), condition=%wide.region_2.3_spmd.clone, body=%wide.region_0.2_spmd.clone.sunk | while | flops 548613504 | bytes 15086155 | solution.py:95
  146.4 1.3 fusion.68
  147.7 0.7 fusion.69
  148.4 0.8 multiply_reduce_fusion.2
  150.2 1.3 fusion.68
  151.6 0.7 fusion.69
  152.3 0.8 multiply_reduce_fusion.2
  154.1 1.3 fusion.68
  155.4 0.7 fusion.69
  156.1 0.8 multiply_reduce_fusion.2
  157.9 1.3 fusion.68
  159.9 0.8 multiply_reduce_fusion.2
  (45 shorter events, 6.4 us)
Async XLA Ops:
  6.5 94.7 %all-gather.2.cloned.1.call-start = ((), (), s32[]{:S(2)}) async-start(), calls=%async_computation.1 | async-start | bytes 6291456 | tf_op jit(solution)/shard_map/all_gather | solution.py:113
  114.4 5.2 %copy-start.1 = (s32[64]{0:T(128)S(1)}, s32[64]{0:T(128)}, u32[]{:S(2)}) copy-start(s32[64]{0:T(128)} %param.15) | copy-start | bytes 772
  115.7 30.0 %all-to-all-start = ((bf16[8,128,1,512]{3,1,2,0:T(8,128)(2,1)}), bf16[8,128,1,512]{3,1,2,0:T(8,128)(2,1)S(1)}, u32[]{:S(2)}, u32[]{:S(2)}) async-start(bf16[8,128,1,512]{3,1,2,0:T(8,128)(2,1)} %pad_maximum_fusion), calls=%async_computation | async-start | bytes 2097152 | tf_op jit(solution)/shard_map/all_to_all | solution.py:102
  160.9 0.7 copy-start
Sparse Core Ops, SparseCore 0:
  8.9 16.3 all-gather.1
where the time goes:
time: 169 us; the launch traced here: 168 us
  blocking collectives  64.5 us (38%)
  other arithmetic  39.6 us (23%)
  waiting for transfers between devices  26 us (15%)
  matrix products  17.2 us (10%)
  between operations  13.5 us (8%)
  starting transfers between devices  3.86 us (2%)
  local copies, waits for them, and re-layouts  3.57 us (2%)
    all_gather x1, blocking collectives, shards(): all_patches = lax.all_gather(patches, 'probe', axis=0, tiled=True)  32.6 us
    convert_element_type x1, other arithmetic, coefficients(): (beam_cos[None, :] * cos_t - beam_sin[None, :] * sin_t).astype(jnp.bfloat16)  28.6 us
    all_gather x1, blocking collectives, shards(): all_pos = lax.all_gather(probe_pos, 'probe', axis=1, tiled=True)  26.2 us
    all_to_all x1, waiting for transfers between devices, apply_patches(): lax.all_to_all(psi_own, 'probe', split_axis=0, concat_axis=2, tiled=True)  25.3 us
    dot_general x1, matrix products, shards(): jnp.einsum('kpb,bcx->kpcx', jnp.stack([real_coef, imag_coef]), full_matri...  13.2 us
    select_n x8, other arithmetic, add_block(): picked = jnp.take(psi, col_ids, axis=1)  5.24 us
    all_to_all x1, starting transfers between devices, apply_patches(): lax.all_to_all(psi_own, 'probe', split_axis=0, concat_axis=2, tiled=True)  3.86 us
    another operation x6, other arithmetic  3.72 us
  transfers between devices with their start and end apart: 2, of which 1 were waited for; matrix products, arithmetic and copies ran while one was open for 18% of the time, Pallas kernels for 0%

commit v1 on v0

--- a/solution.py
+++ b/solution.py
@@ -106,7 +106,21 @@
 def shards(smatrix, aperture, aberration, beam_k, probe_pos, patches, patch_col):
     probe_count = lax.axis_size("probe")
     beam_count = lax.axis_size("beam")
-    all_patches = lax.all_gather(patches, "probe", axis=0, tiled=True)
+    world = lax.axis_size("probe")
+    blocks_here = [(i0, (i0 + 1) % world) for i0 in range(world)]
+    seen = [(i0, (i0 - 1) % world) for i0 in range(world)]
+    then, front = ([patches], [patches])
+    for _ in range(world // 2):
+        y1 = lax.ppermute(then[-1], perm=blocks_here, axis_name="probe")
+        then.append(y1)
+    it = 0
+    while it < (world - 1) // 2:
+        even = lax.ppermute(front[-1], axis_name="probe", perm=seen)
+        front.append(even)
+        it = it + 1
+    now = jnp.concatenate([*then[::-1], *front[1:]], 0)
+    plain = lax.axis_index("probe")
+    all_patches = jnp.roll(now, (plain - world // 2) * patches.shape[0], 0)
     det_table = detector(PSIDE)
     col_dev = smatrix.shape[1]
     width_two = smatrix.shape[2]

time: 169 us -> 154 us (0.911)
  blocking collectives: 64.5 us -> 32 us
  starting transfers between devices: 3.86 us -> 20.1 us
    all_gather x1 -> x0, blocking collectives: 32.6 us -> none  [shards(): all_patches = lax.all_gather(patches, 'probe', axis=0, tiled=True)]
    ppermute x0 -> x7, starting transfers between devices: none -> 13.9 us  [the longest x3 10.8 us: shards(): even = lax.ppermute(front[-1], axis_name='probe', perm=seen)]
    ppermute x0 -> x7, waiting for transfers between devices: none -> 6.2 us  [the longest x4 5.55 us: shards(): y1 = lax.ppermute(then[-1], perm=blocks_here, axis_name='probe')]
    all_to_all x1, waiting for transfers between devices: 25.3 us -> 19.8 us  [apply_patches(): lax.all_to_all(psi_own, 'probe', split_axis=0, concat_axis=2, tiled=True)]
    all_to_all x1, starting transfers between devices: 3.86 us -> 6.26 us  [apply_patches(): lax.all_to_all(psi_own, 'probe', split_axis=0, concat_axis=2, tiled=True)]
  transfers between devices with their start and end apart: 2 -> 9, of which waited for: 1 -> 3; matrix products, arithmetic and copies ran while one was open for 18% -> 21% of each run, Pallas kernels for 0% -> 0%
where the time goes in v1:
time: 154 us
  other arithmetic  39.6 us (26%)
  blocking collectives  32 us (21%)
  waiting for transfers between devices  26.1 us (17%)
  starting transfers between devices  20.1 us (13%)
  matrix products  17.2 us (11%)
  between operations  13.5 us (9%)
  local copies, waits for them, and re-layouts  5.01 us (3%)
    convert_element_type x1, other arithmetic, coefficients(): (beam_cos[None, :] * cos_t - beam_sin[None, :] * sin_t).astype(jnp.bfloat16)  28.6 us
    all_gather x1, blocking collectives, shards(): all_pos = lax.all_gather(probe_pos, 'probe', axis=1, tiled=True)  26.3 us
    all_to_all x1, waiting for transfers between devices, apply_patches(): lax.all_to_all(psi_own, 'probe', split_axis=0, concat_axis=2, tiled=True)  19.8 us
    dot_general x1, matrix products, shards(): jnp.einsum('kpb,bcx->kpcx', jnp.stack([real_coef, imag_coef]), full_matri...  13.2 us
    ppermute x3, starting transfers between devices, shards(): even = lax.ppermute(front[-1], axis_name='probe', perm=seen)  10.8 us
    all_to_all x1, starting transfers between devices, apply_patches(): lax.all_to_all(psi_own, 'probe', split_axis=0, concat_axis=2, tiled=True)  6.26 us
    ppermute x4, waiting for transfers between devices, shards(): y1 = lax.ppermute(then[-1], perm=blocks_here, axis_name='probe')  5.55 us
    select_n x8, other arithmetic, add_block(): picked = jnp.take(psi, col_ids, axis=1)  5.24 us
  transfers between devices with their start and end apart: 9, of which 3 were waited for; matrix products, arithmetic and copies ran while one was open for 21% of the time, Pallas kernels for 0%

profile of v1, /device:TPU:0, one launch (start us, length us, event | category | flops | bytes accessed | tf_op | source)
XLA Modules:
  0.0 153.8 jit_solution(12578288067323097044)
XLA Ops:
  6.5 3.0 %collective-permute-start = (bf16[8,512]{1,0:T(8,128)(2,1)}, bf16[8,512]{1,0:T(8,128)(2,1)S(1)}, u32[]{:S(2)}, u32[]{:S(2)}) collective-permute-start(bf16[8,512]{1,0:T(8,128)(2,1)} %param.14), channel_id=1, source_target_pairs={{0,2},{2,4},{4,6},{6,8},{8,10},{10,12},{12,14},{14,0},{1,3},{3,5},... | collective-permute-start | bytes 24584 | tf_op jit(solution)/shard_map/ppermute | solution.py:114
  9.5 3.0 %collective-permute-start.4 = (bf16[8,512]{1,0:T(8,128)(2,1)}, bf16[8,512]{1,0:T(8,128)(2,1)S(1)}, u32[]{:S(2)}, u32[]{:S(2)}) collective-permute-start(bf16[8,512]{1,0:T(8,128)(2,1)} %param.14), channel_id=1, source_target_pairs={{0,14},{2,0},{4,2},{6,4},{8,6},{10,8},{12,10},{14,12},{1,15},{3,1}... | collective-permute-start | bytes 24584 | tf_op jit(solution)/shard_map/ppermute | solution.py:118
  12.6 2.0 %all_gather.17 = s32[2,4096]{1,0:T(2,128)S(1)} all-gather(s32[2,2048]{1,0:T(2,128)} %param.12), channel_id=1, replica_groups=mesh['grp'=2,'probe'=8,'beam'=2] {'beam'}, dimensions={1}, use_global_device_ids=true | all-gather | bytes 49152 | tf_op jit(solution)/shard_map/all_gather | solution.py:130
  14.7 0.8 cosine_multiply_fusion
  15.5 5.5 %collective-permute-done.1 = bf16[8,512]{1,0:T(8,128)(2,1)S(1)} collective-permute-done((bf16[8,512]{1,0:T(8,128)(2,1)S(1)}, bf16[8,512]{1,0:T(8,128)(2,1)S(1)}, u32[]{:S(2)}, u32[]{:S(2)}) %collective-permute-start.1) | collective-permute-done | bytes 8224 | tf_op jit(solution)/shard_map/ppermute | solution.py:114
  21.1 1.8 %all_gather.15 = f32[4096]{0:T(1024)S(1)} all-gather(f32[2048]{0:T(1024)S(1)} %get-tuple-element.96), channel_id=1, replica_groups=mesh['grp'=2,'probe'=8,'beam'=2] {'beam'}, dimensions={0}, use_global_device_ids=true | all-gather | bytes 24576 | tf_op jit(solution)/shard_map/all_gather | solution.py:128
  22.9 1.8 %all_gather.18 = f32[4096]{0:T(1024)S(1)} all-gather(f32[2048]{0:T(1024)S(1)} %get-tuple-element.97), channel_id=1, replica_groups=mesh['grp'=2,'probe'=8,'beam'=2] {'beam'}, dimensions={0}, use_global_device_ids=true | all-gather | bytes 24576 | tf_op jit(solution)/shard_map/all_gather | solution.py:129
  24.7 4.8 %collective-permute-start.5 = (bf16[8,512]{1,0:T(8,128)(2,1)S(1)}, bf16[8,512]{1,0:T(8,128)(2,1)S(1)}, u32[]{:S(2)}, u32[]{:S(2)}) collective-permute-start(bf16[8,512]{1,0:T(8,128)(2,1)S(1)} %collective-permute-done.4), channel_id=1, source_target_pairs={{0,14},{2,0},{4,2},{6,4},{8,6},{10,8},{12,10},{14,12},{1,15},{3,1}... | collective-permute-start | bytes 24584 | tf_op jit(solution)/shard_map/ppermute | solution.py:118
  29.5 26.3 %all_gather.16 = s32[2,2048]{1,0:T(2,128)S(1)} all-gather(s32[2,256]{1,0:T(2,128)} %param.13), channel_id=1, replica_groups=mesh['grp'=2,'probe'=8,'beam'=2] {'probe'}, dimensions={1}, use_global_device_ids=true | all-gather | bytes 18432 | tf_op jit(solution)/shard_map/all_gather | solution.py:131
  55.8 3.0 %collective-permute-start.6 = (bf16[8,512]{1,0:T(8,128)(2,1)S(1)}, bf16[8,512]{1,0:T(8,128)(2,1)S(1)}, u32[]{:S(2)}, u32[]{:S(2)}) collective-permute-start(bf16[8,512]{1,0:T(8,128)(2,1)S(1)} %collective-permute-done.5), channel_id=1, source_target_pairs={{0,14},{2,0},{4,2},{6,4},{8,6},{10,8},{12,10},{14,12},{1,15},{3,1}... | collective-permute-start | bytes 24584 | tf_op jit(solution)/shard_map/ppermute | solution.py:118
  61.0 28.6 %subtract_convert_fusion = (bf16[1,1024,4096]{2,1,0:T(8,128)(2,1)}, bf16[1,1024,4096]{2,1,0:T(8,128)(2,1)}) fusion(f32[4096]{0:T(1024)S(1)} %all_gather.18, f32[4096]{0:T(1024)S(1)} %all_gather.15, s32[4096]{0:T(1024)S(1)} %bitcast.53, s32[1024]{0:T(1024)S(1)} %bitcast.55, s32[4096]{0:T(1024)S(1)} %bitcast.52, s32[1024]{0:T(1024)S(1)} %bitcast.54), kind=kLoop, calls=%fused_computation.60 | loop fusion | flops 209715200 | bytes 16850944 | tf_op jit(solution)/shard_map/convert_element_type | solution.py:29
  89.6 13.2 %fusion.37 = f32[2,1024,1,512]{3,1,0,2:T(8,128)S(1)} fusion(bf16[4096,1,512]{2,0,1:T(8,128)(2,1)} %all-gather.2.cloned.1.call-done, bf16[1,1024,4096]{2,1,0:T(8,128)(2,1)} %get-tuple-element.91, bf16[1,1024,4096]{2,1,0:T(8,128)(2,1)} %get-tuple-element.90), kind=kOutput, calls=%fused_computation.68 | convolution fusion | flops 8598323200 | bytes 25165824 | tf_op jit(solution)/shard_map/kpb,bcx->kpcx/dot_general | solution.py:140
  103.1 1.1 pad_maximum_fusion
  104.1 6.3 %all-to-all-start = ((bf16[8,128,1,512]{3,1,2,0:T(8,128)(2,1)}), bf16[8,128,1,512]{3,1,2,0:T(8,128)(2,1)S(1)}, u32[]{:S(2)}, u32[]{:S(2)}) async-start(bf16[8,128,1,512]{3,1,2,0:T(8,128)(2,1)} %pad_maximum_fusion), calls=%async_computation | async-start | bytes 2097152 | tf_op jit(solution)/shard_map/all_to_all | solution.py:102
  111.2 19.8 %all-to-all-done = bf16[8,128,1,512]{3,1,2,0:T(8,128)(2,1)S(1)} async-done(((bf16[8,128,1,512]{3,1,2,0:T(8,128)(2,1)}), bf16[8,128,1,512]{3,1,2,0:T(8,128)(2,1)S(1)}, u32[]{:S(2)}, u32[]{:S(2)}) %all-to-all-start) | async-done | bytes 1048608 | tf_op jit(solution)/shard_map/all_to_all | solution.py:102
  131.0 15.3 %while.11 = (s32[]{:T(128)}, f32[8,128]{1,0:T(8,128)S(1)}, s32[4,16]{1,0:T(4,128)S(1)}, bf16[128,8,512]{2,0,1:T(8,128)(2,1)S(1)}, bf16[4,16,512]{2,1,0:T(8,128)(...) while((s32[]{:T(128)}, f32[8,128]{1,0:T(8,128)S(1)}, s32[4,16]{1,0:T(4,128)S(1)}, ...), condition=%wide.region_2.3_spmd.clone, body=%wide.region_0.2_spmd.clone.sunk | while | flops 548613504 | bytes 15086155 | solution.py:95
  131.8 1.3 fusion.68
  133.8 0.8 multiply_reduce_fusion.2
  135.6 1.3 fusion.68
  137.6 0.8 multiply_reduce_fusion.2
  139.4 1.3 fusion.68
  141.5 0.8 multiply_reduce_fusion.2
  143.3 1.3 fusion.68
  145.3 0.8 multiply_reduce_fusion.2
  (75 shorter events, 10.6 us)
Async XLA Ops:
  6.5 83.1 %all-gather.2.cloned.1.call-start = ((), (), s32[]{:S(2)}) async-start(), calls=%async_computation.1 | async-start | bytes 6291456 | tf_op jit(solution)/shard_map/all_gather | solution.py:127
  6.5 8.1 %collective-permute-start = (bf16[8,512]{1,0:T(8,128)(2,1)}, bf16[8,512]{1,0:T(8,128)(2,1)S(1)}, u32[]{:S(2)}, u32[]{:S(2)}) collective-permute-start(bf16[8,512]{1,0:T(8,128)(2,1)} %param.14), channel_id=1, source_target_pairs={{0,2},{2,4},{4,6},{6,8},{8,10},{10,12},{12,14},{14,0},{1,3},{3,5},... | collective-permute-start | bytes 24584 | tf_op jit(solution)/shard_map/ppermute | solution.py:114
  9.5 15.2 %collective-permute-start.4 = (bf16[8,512]{1,0:T(8,128)(2,1)}, bf16[8,512]{1,0:T(8,128)(2,1)S(1)}, u32[]{:S(2)}, u32[]{:S(2)}) collective-permute-start(bf16[8,512]{1,0:T(8,128)(2,1)} %param.14), channel_id=1, source_target_pairs={{0,14},{2,0},{4,2},{6,4},{8,6},{10,8},{12,10},{14,12},{1,15},{3,1}... | collective-permute-start | bytes 24584 | tf_op jit(solution)/shard_map/ppermute | solution.py:118
  14.7 6.4 %collective-permute-start.1 = (bf16[8,512]{1,0:T(8,128)(2,1)S(1)}, bf16[8,512]{1,0:T(8,128)(2,1)S(1)}, u32[]{:S(2)}, u32[]{:S(2)}) collective-permute-start(bf16[8,512]{1,0:T(8,128)(2,1)S(1)} %collective-permute-done), channel_id=1, source_target_pairs={{0,2},{2,4},{4,6},{6,8},{8,10},{10,12},{12,14},{14,0},{1,3},{3,5},... | collective-permute-start | bytes 24584 | tf_op jit(solution)/shard_map/ppermute | solution.py:114
  21.1 8.4 %collective-permute-start.2 = (bf16[8,512]{1,0:T(8,128)(2,1)S(1)}, bf16[8,512]{1,0:T(8,128)(2,1)S(1)}, u32[]{:S(2)}, u32[]{:S(2)}) collective-permute-start(bf16[8,512]{1,0:T(8,128)(2,1)S(1)} %collective-permute-done.1), channel_id=1, source_target_pairs={{0,2},{2,4},{4,6},{6,8},{8,10},{10,12},{12,14},{14,0},{1,3},{3,5},... | collective-permute-start | bytes 24584 | tf_op jit(solution)/shard_map/ppermute | solution.py:114
  24.7 31.1 %collective-permute-start.5 = (bf16[8,512]{1,0:T(8,128)(2,1)S(1)}, bf16[8,512]{1,0:T(8,128)(2,1)S(1)}, u32[]{:S(2)}, u32[]{:S(2)}) collective-permute-start(bf16[8,512]{1,0:T(8,128)(2,1)S(1)} %collective-permute-done.4), channel_id=1, source_target_pairs={{0,14},{2,0},{4,2},{6,4},{8,6},{10,8},{12,10},{14,12},{1,15},{3,1}... | collective-permute-start | bytes 24584 | tf_op jit(solution)/shard_map/ppermute | solution.py:118
  29.5 29.3 %collective-permute-start.3 = (bf16[8,512]{1,0:T(8,128)(2,1)S(1)}, bf16[8,512]{1,0:T(8,128)(2,1)S(1)}, u32[]{:S(2)}, u32[]{:S(2)}) collective-permute-start(bf16[8,512]{1,0:T(8,128)(2,1)S(1)} %collective-permute-done.2), channel_id=1, source_target_pairs={{0,2},{2,4},{4,6},{6,8},{8,10},{10,12},{12,14},{14,0},{1,3},{3,5},... | collective-permute-start | bytes 24584 | tf_op jit(solution)/shard_map/ppermute | solution.py:114
  55.8 4.4 %collective-permute-start.6 = (bf16[8,512]{1,0:T(8,128)(2,1)S(1)}, bf16[8,512]{1,0:T(8,128)(2,1)S(1)}, u32[]{:S(2)}, u32[]{:S(2)}) collective-permute-start(bf16[8,512]{1,0:T(8,128)(2,1)S(1)} %collective-permute-done.5), channel_id=1, source_target_pairs={{0,14},{2,0},{4,2},{6,4},{8,6},{10,8},{12,10},{14,12},{1,15},{3,1}... | collective-permute-start | bytes 24584 | tf_op jit(solution)/shard_map/ppermute | solution.py:118
  102.8 7.6 %copy-start.1 = (s32[64]{0:T(128)S(1)}, s32[64]{0:T(128)}, u32[]{:S(2)}) copy-start(s32[64]{0:T(128)} %param.15) | copy-start | bytes 772
  104.1 26.9 %all-to-all-start = ((bf16[8,128,1,512]{3,1,2,0:T(8,128)(2,1)}), bf16[8,128,1,512]{3,1,2,0:T(8,128)(2,1)S(1)}, u32[]{:S(2)}, u32[]{:S(2)}) async-start(bf16[8,128,1,512]{3,1,2,0:T(8,128)(2,1)} %pad_maximum_fusion), calls=%async_computation | async-start | bytes 2097152 | tf_op jit(solution)/shard_map/all_to_all | solution.py:102
  146.3 0.7 copy-start
Sparse Core Ops, SparseCore 0:
  12.7 12.5 all-gather.1
